TPU v7x, 128 devices: a whole 4x4x4 slice. The times are simulated.
128 devices in a mesh: dp: 8 (over z, core), label: 16 (over x, y).
Axes of the slice: x: 4, y: 4, z: 4, core: 2. Of those that a mesh axis runs over, the one named last changes fastest.
Arguments:
- features: bfloat16 [262144, 768], P(('dp', 'label')), may hold values from -6 to 6
- inst_ids: int32 [2048, 4], P(('dp', 'label')), may hold values from 0 to 15
- lab_ids: int32 [2048, 4], P(('dp', 'label')), may hold values from 0 to 15
- counts: int32 [2048], P(('dp', 'label')), may hold values from 0 to 4, as said below
- block_bits: int32 [2048, 4, 128, 128], P(('dp', 'label')), may hold values 0 or 1
- centroids: bfloat16 [2048, 768], P('label'), may hold values from -40 to 40
Outputs:
- label_embed: bfloat16 [32768, 768], P(('dp', 'label'))
- membership: bfloat16 [32768, 2048], P(('dp', 'label'))
- targets: bfloat16 [262144, 768], P(('dp', 'label'))
Inputs may be any that keep to these rules, and one draw needn't show every extreme that they name: `lab_ids`: label block within the slot's label column. `counts`: in every draw one label column has all 4 slots used on every device.
All inputs are finite; a program needn't handle non-finite values. No bound on the sum of `block_bits` on one device may be relied on, other than what follows from the above.
Results may differ from a plain program's by a relative error of at most 0.008.
The roundings to bfloat16 on the way count: a program that leaves them out, or rounds other values in their place, can miss the bound.
Values may be sent and summed in bfloat16 or wider, within the bound.
No kernel may reach another device: no remote copies, remote signals or barrier semaphores. Data moves between devices by JAX's collectives and lax.ppermute only.
A program may use at most 128 MiB of HBM per device.

v0:
```python
import jax
import jax.numpy as jnp
from jax import lax
from jax.sharding import PartitionSpec as P

LB_DEV = 2
epsilon = 1e-05


def label_side(column_sums, centroids):
    embed32 = column_sums * lax.rsqrt(
        jnp.mean(column_sums * column_sums, axis=1, keepdims=True) + epsilon
    )
    label_embed = embed32.astype(jnp.bfloat16)
    all_rows = lax.all_gather(centroids, "label", axis=0, tiled=True)
    scores = jnp.einsum("rd,kd->rk", label_embed, all_rows, preferred_element_type=jnp.float32)
    row_peak = jnp.max(scores, axis=1, keepdims=True)
    lifted = jnp.exp(scores - row_peak)
    membership = (lifted / jnp.sum(lifted, axis=1, keepdims=True)).astype(jnp.bfloat16)
    mixed_rows = jnp.dot(membership, all_rows, preferred_element_type=jnp.float32)
    return (label_embed, membership, mixed_rows.astype(jnp.bfloat16))


def body(features, inst_ids, lab_ids, counts, block_bits, centroids):
    dest_count, slot_cap = inst_ids.shape
    block_size = block_bits.shape[-1]
    feat_width = features.shape[1]
    inst_blocks = features.reshape(-1, block_size, feat_width)
    gathered = inst_blocks[inst_ids]
    incidence = block_bits.astype(jnp.bfloat16)
    partials = jnp.einsum(
        "ncab,ncad->ncbd", incidence, gathered, preferred_element_type=jnp.float32
    ).astype(jnp.bfloat16)
    filled = jnp.arange(slot_cap)[None, :] < counts[:, None]
    tagged_ids = jnp.where(filled, lab_ids, -1)
    arrived, arrived_ids = (
        lax.all_to_all(partials, "label", split_axis=0, concat_axis=0, tiled=True),
        lax.all_to_all(tagged_ids, "label", split_axis=0, concat_axis=0, tiled=True),
    )
    share_rows = LB_DEV * block_size
    col_blocks = lax.axis_size("dp") * LB_DEV
    slot_total = dest_count * slot_cap
    flat_ids = arrived_ids.reshape(slot_total)
    selector = (flat_ids[None, :] == jnp.arange(col_blocks)[:, None]).astype(jnp.bfloat16)
    column_sums = jnp.dot(
        selector,
        arrived.reshape(slot_total, block_size * feat_width),
        preferred_element_type=jnp.float32,
    )
    column_total = lax.psum(column_sums, "dp")
    embed_all, member_all, column_mixed = label_side(
        column_total.reshape(col_blocks * block_size, feat_width), centroids
    )
    offset = lax.axis_index("dp") * share_rows
    label_embed = lax.dynamic_slice_in_dim(embed_all, offset, share_rows, 0)
    membership = lax.dynamic_slice_in_dim(member_all, offset, share_rows, 0)
    mixed_blocks = column_mixed.reshape(col_blocks, block_size, feat_width)
    picked = mixed_blocks[jnp.maximum(arrived_ids, 0)]
    picked = jnp.where((arrived_ids >= 0)[:, :, None, None], picked, jnp.zeros_like(picked))
    returned = lax.all_to_all(picked, "label", split_axis=0, concat_axis=0, tiled=True)
    contrib = jnp.einsum("ncab,ncbd->ncad", incidence, returned, preferred_element_type=jnp.float32)
    owner_map = (
        inst_ids.reshape(slot_total)[None, :] == jnp.arange(inst_blocks.shape[0])[:, None]
    ).astype(jnp.float32)
    raw_targets = jnp.dot(
        owner_map,
        contrib.reshape(slot_total, block_size * feat_width),
        precision=lax.Precision.HIGHEST,
    )
    raw_targets = raw_targets.reshape(-1, feat_width)
    targets = raw_targets * lax.rsqrt(
        jnp.mean(raw_targets * raw_targets, axis=1, keepdims=True) + epsilon
    )
    return (label_embed, membership, targets.astype(jnp.bfloat16))


def solution(mesh):
    in_specs = (
        P(("dp", "label"), None),
        P(("dp", "label"), None),
        P(("dp", "label"), None),
        P(("dp", "label")),
        P(("dp", "label"), None, None, None),
        P("label", None),
    )
    out_specs = (P(("dp", "label"), None), P(("dp", "label"), None), P(("dp", "label"), None))
    return jax.shard_map(body, mesh=mesh, in_specs=in_specs, out_specs=out_specs, check_vma=False)
```

profile of v0, /device:TPU:61, one launch (start us, length us, event | category | flops | bytes accessed | tf_op | source)
XLA Modules:
  0.0 778.2 jit_solution(7269517425034337055)
XLA Ops:
  8.0 0.8 select_bitcast_fusion
  9.5 6.6 all-to-all-start
  17.0 7.3 gather_fusion
  24.3 10.8 %convert_bitcast_fusion = bf16[16,4,128,768]{2,3,1,0:T(8,128)(2,1)} fusion(bf16[16,4,128,768]{3,2,1,0:T(8,128)(2,1)} %bitcast.31, s32[16,4,128,128]{3,2,1,0:T(8,128)} %param.10), kind=kOutput, calls=%fused_computation.5 | convolution fusion | flops 1617952768 | bytes 29360128 | tf_op jit(solution)/shard_map/ncab,ncad->ncbd/dot_general | solution.py:31
  35.1 6.7 all-to-all-start.1
  42.3 0.7 maximum_reduce_fusion
  43.1 219.6 %all-to-all-done.1 = bf16[16,4,128,768]{2,3,1,0:T(8,128)(2,1)} async-done(((bf16[16,4,128,768]{2,3,1,0:T(8,128)(2,1)}), bf16[16,4,128,768]{2,3,1,0:T(8,128)(2,1)}, u32[]{:S(2)}, u32[]{:S(2)}) %all-to-all-start.1) | async-done | bytes 12582944 | tf_op jit(solution)/shard_map/all_to_all | solution.py:37
  262.7 16.7 %copy.37 = bf16[8,8,128,768]{3,1,2,0:T(8,128)(2,1)} copy(bf16[8,8,128,768]{2,3,1,0:T(8,128)(2,1)} %bitcast.18) | data formatting | bytes 25165824
  279.4 9.0 %fusion.3 = f32[16,98304]{1,0:T(8,128)} fusion(bf16[64,98304]{1,0:T(8,128)(2,1)} %bitcast.34, s32[64]{0:T(128)S(1)} %eq.30), kind=kOutput, calls=%fused_computation.20 | convolution fusion | flops 201327616 | bytes 18874624 | tf_op jit(solution)/shard_map/dot_general | solution.py:45
  288.4 5.0 reshape.69
  294.3 91.9 %all-reduce.2.cloned.1.call-done = f32[2048,768]{1,0:T(8,128)} async-done(((f32[2048,768]{1,0:T(8,128)}), f32[2048,768]{1,0:T(8,128)}) %all-reduce.2.cloned.1.call-update) | async-done | bytes 6291472 | tf_op jit(solution)/shard_map/psum | solution.py:50
  386.2 3.4 multiply_reduce_fusion.1
  389.6 1.2 copy-done.3
  391.2 13.1 %fusion.7 = (f32[2048]{0:T(1024)S(1)}, f32[2048,2048]{0,1:T(8,128)}) fusion(bf16[2048,768]{1,0:T(8,128)(2,1)S(1)} %multiply_convert_fusion.1, bf16[2048,768]{1,0:T(8,128)(2,1)} %all-gather.2.cloned.1.call-done), kind=kOutput, calls=%fused_computation.32 | convolution fusion | flops 6446643200 | bytes 23076864 | tf_op jit(solution)/shard_map/rd,kd->rk/dot_general | solution.py:16
  404.4 8.1 %fusion = f32[2048]{0:T(1024)S(1)} fusion(f32[2048,2048]{0,1:T(8,128)} %get-tuple-element.15, f32[2048]{0:T(1024)S(1)} %get-tuple-element.14), kind=kLoop, calls=%fused_computation.4 | loop fusion | flops 8386560 | bytes 16793600 | tf_op jit(solution)/shard_map/reduce_sum | solution.py:19
  412.4 7.5 divide_convert_fusion
  419.9 7.3 convolution_convert_fusion
  427.3 7.1 gather_fusion.1
  434.4 16.6 %copy.34 = bf16[64,128,768]{1,2,0:T(8,128)(2,1)} copy(bf16[64,128,768]{2,1,0:T(8,128)(2,1)} %gather_fusion.1) | data formatting | bytes 25165824 | tf_op jit(solution)/shard_map/gather | solution.py:58
  451.0 10.6 %broadcast_select_fusion = bf16[16,4,128,768]{2,3,1,0:T(8,128)(2,1)} fusion(bf16[16,4,128,768]{2,3,1,0:T(8,128)(2,1)} %bitcast.32, pred[16,4]{1,0:T(8,128)(4,1)S(1)} %copy.33), kind=kLoop, calls=%fused_computation.6 | loop fusion | flops 6291456 | bytes 25165888 | tf_op jit(solution)/shard_map/jit(_where)/select_n | solution.py:59
  461.7 6.9 all-to-all-start.2
  468.7 1.3 constant_dynamic-slice_fusion
  470.0 1.4 copy.36
  471.4 1.8 constant_dynamic-slice_fusion.1
  473.2 232.2 %all-to-all-done.2 = bf16[16,4,128,768]{2,3,1,0:T(8,128)(2,1)} async-done(((bf16[16,4,128,768]{2,3,1,0:T(8,128)(2,1)}), bf16[16,4,128,768]{2,3,1,0:T(8,128)(2,1)}, u32[]{:S(2)}, u32[]{:S(2)}) %all-to-all-start.2) | async-done | bytes 12582944 | tf_op jit(solution)/shard_map/all_to_all | solution.py:60
  705.4 14.1 %convolution_bitcast_fusion = f32[16,4,128,768]{2,3,1,0:T(8,128)} fusion(bf16[16,4,128,768]{2,3,1,0:T(8,128)(2,1)} %all-to-all-done.2, s32[16,4,128,128]{3,2,1,0:T(8,128)} %param.10), kind=kOutput, calls=%fused_computation.7 | convolution fusion | flops 1611661312 | bytes 41943040 | tf_op jit(solution)/shard_map/ncab,ncbd->ncad/dot_general | solution.py:61
  719.5 25.1 %copy.38 = f32[8,8,128,768]{3,1,2,0:T(8,128)} copy(f32[8,8,128,768]{2,3,1,0:T(8,128)} %bitcast.29) | data formatting | bytes 50331648
  744.6 14.3 %fusion.4 = f32[16,98304]{1,0:T(8,128)} fusion(f32[64,98304]{1,0:T(8,128)} %bitcast.30, s32[64]{0:T(128)S(1)} %eq.34), kind=kOutput, calls=%fused_computation.21 | convolution fusion | flops 1207960576 | bytes 31457536 | tf_op jit(solution)/shard_map/dot_general | solution.py:65
  758.9 5.2 reshape.72
  764.1 3.4 multiply_reduce_fusion
  767.5 1.2 copy-done.2
  768.7 2.1 multiply_convert_fusion
  (37 shorter events, 3.7 us)
Async XLA Ops:
  8.0 9.0 %copy-start = (bf16[2048,768]{1,0:T(8,128)(2,1)S(1)}, bf16[2048,768]{1,0:T(8,128)(2,1)}, u32[]{:S(2)}) copy-start(bf16[2048,768]{1,0:T(8,128)(2,1)} %param.6) | copy-start | bytes 9437188
  9.5 25.5 %all-to-all-start = ((s32[16,1,4]{2,1,0:T(1,128)}), s32[16,1,4]{2,1,0:T(1,128)S(1)}, u32[]{:S(2)}, u32[]{:S(2)}) async-start(s32[16,1,4]{2,1,0:T(1,128)} %copy.27), calls=%async_computation | async-start | bytes 16384 | tf_op jit(solution)/shard_map/all_to_all | solution.py:38
  35.1 227.6 %all-to-all-start.1 = ((bf16[16,4,128,768]{2,3,1,0:T(8,128)(2,1)}), bf16[16,4,128,768]{2,3,1,0:T(8,128)(2,1)}, u32[]{:S(2)}, u32[]{:S(2)}) async-start(bf16[16,4,128,768]{2,3,1,0:T(8,128)(2,1)} %convert_bitcast_fusion), calls=%async_computation.1 | async-start | bytes 25165824 | tf_op jit(solution)/shard_map/all_to_all | solution.py:37
  41.7 344.4 %all-reduce.2.cloned.1.call-start = ((), (), s32[]{:S(2)}) async-start(), calls=%async_computation.3 | async-start | bytes 12582912 | tf_op jit(solution)/shard_map/psum | solution.py:50
  293.4 97.8 %all-gather.2.cloned.1.call-start = ((), (), s32[]{:S(2)}) async-start(), calls=%async_computation.4 | async-start | bytes 3342336 | tf_op jit(solution)/shard_map/all_gather | solution.py:15
  386.2 4.6 copy-start.3
  391.2 13.2 %copy-start.5 = (bf16[2048,768]{1,0:T(8,128)(2,1)}, bf16[2048,768]{1,0:T(8,128)(2,1)S(1)}, u32[]{:S(2)}) copy-start(bf16[2048,768]{1,0:T(8,128)(2,1)S(1)} %multiply_convert_fusion.1) | copy-start | bytes 9437188
  412.4 7.5 copy-start.7
  419.9 7.3 copy-start.4
  461.7 6.9 copy-start.6
  461.7 243.7 %all-to-all-start.2 = ((bf16[16,4,128,768]{2,3,1,0:T(8,128)(2,1)}), bf16[16,4,128,768]{2,3,1,0:T(8,128)(2,1)}, u32[]{:S(2)}, u32[]{:S(2)}) async-start(bf16[16,4,128,768]{2,3,1,0:T(8,128)(2,1)} %broadcast_select_fusion), calls=%async_computation.2 | async-start | bytes 25165824 | tf_op jit(solution)/shard_map/all_to_all | solution.py:60
  758.9 11.8 %copy-start.1 = (bf16[2048,768]{1,0:T(8,128)(2,1)S(1)}, bf16[2048,768]{1,0:T(8,128)(2,1)}, u32[]{:S(2)}) copy-start(bf16[2048,768]{1,0:T(8,128)(2,1)} %param.6) | copy-start | bytes 9437188
  764.1 4.6 copy-start.2
Sparse Core Ops, SparseCore 0:
  293.5 92.5 all-reduce.1
Sparse Core Ops, SparseCore 1:
  296.1 53.1 all-gather.1
where the time goes:
time: 780 us; the launch traced here: 778 us
  waiting for transfers between devices  544 us (70%)
  local copies, waits for them, and re-layouts  91.8 us (12%)
  matrix products  68.7 us (9%)
  other arithmetic  37.7 us (5%)
  starting transfers between devices  20.2 us (3%)
  between operations  15.6 us (2%)
    all_to_all x1, waiting for transfers between devices, body(): lax.all_to_all(picked, 'label', split_axis=0, concat_axis=0, tiled=True)  232 us
    all_to_all x1, waiting for transfers between devices, body(): lax.all_to_all(partials, 'label', split_axis=0, concat_axis=0, tiled=True)  220 us
    psum x1, waiting for transfers between devices, body(): column_total = lax.psum(column_sums, 'dp')  91.9 us
    unnamed x20, local copies, waits for them, and re-layouts  45.7 us
    gather x2, local copies, waits for them, and re-layouts, body(): picked = mixed_blocks[jnp.maximum(arrived_ids, 0)]  23.8 us
  transfers between devices with their start and end apart: 5, of which 3 were waited for; matrix products, arithmetic and copies ran while one was open for 4% of the time, Pallas kernels for 0%

commit v1 on v0

--- a/solution.py
+++ b/solution.py
@@ -47,7 +47,7 @@
         arrived.reshape(slot_total, block_size * feat_width),
         preferred_element_type=jnp.float32,
     )
-    column_total = lax.psum(column_sums, "dp")
+    column_total = jnp.sum(lax.all_gather(column_sums, "dp"), axis=0)
     embed_all, member_all, column_mixed = label_side(
         column_total.reshape(col_blocks * block_size, feat_width), centroids
     )

time: 780 us -> 950 us (1.22)
  waiting for transfers between devices: 544 us -> 687 us
  other arithmetic: 37.7 us -> 57.9 us
    all_gather x0 -> x1, waiting for transfers between devices: none -> 234 us  [body(): column_total = jnp.sum(lax.all_gather(column_sums, 'dp'), axis=0)]
    psum x1 -> x0, waiting for transfers between devices: 91.9 us -> none  [body(): column_total = lax.psum(column_sums, 'dp')]
    reduce_sum x0 -> x1, other arithmetic: none -> 20.2 us  [body(): column_total = jnp.sum(lax.all_gather(column_sums, 'dp'), axis=0)]
    all_gather x1, waiting for transfers between devices: 0.03 us -> 17.4 us  [label_side(): all_rows = lax.all_gather(centroids, 'label', axis=0, tiled=True)]
    all_to_all x1, waiting for transfers between devices: 232 us -> 215 us  [body(): lax.all_to_all(picked, 'label', split_axis=0, concat_axis=0, tiled=True)]
  transfers between devices with their start and end apart: 5 -> 5, of which waited for: 3 -> 4; matrix products, arithmetic and copies ran while one was open for 4% -> 6% of each run, Pallas kernels for 0% -> 0%
where the time goes in v1:
time: 950 us; the launch traced here: 939 us
  waiting for transfers between devices  687 us (72%)
  local copies, waits for them, and re-layouts  92 us (10%)
  matrix products  67.4 us (7%)
  other arithmetic  57.9 us (6%)
  starting transfers between devices  20.9 us (2%)
  between operations  14.2 us (1%)
    all_gather x1, waiting for transfers between devices, body(): column_total = jnp.sum(lax.all_gather(column_sums, 'dp'), axis=0)  234 us
    all_to_all x1, waiting for transfers between devices, body(): lax.all_to_all(partials, 'label', split_axis=0, concat_axis=0, tiled=True)  220 us
    all_to_all x1, waiting for transfers between devices, body(): lax.all_to_all(picked, 'label', split_axis=0, concat_axis=0, tiled=True)  215 us
    unnamed x20, local copies, waits for them, and re-layouts  45.7 us
    gather x2, local copies, waits for them, and re-layouts, body(): picked = mixed_blocks[jnp.maximum(arrived_ids, 0)]  24 us
    reduce_sum x1, other arithmetic, body(): column_total = jnp.sum(lax.all_gather(column_sums, 'dp'), axis=0)  20.2 us
  transfers between devices with their start and end apart: 5, of which 4 were waited for; matrix products, arithmetic and copies ran while one was open for 6% of the time, Pallas kernels for 0%

profile of v1, /device:TPU:61, one launch (start us, length us, event | category | flops | bytes accessed | tf_op | source)
XLA Modules:
  0.0 939.1 jit_solution(260971121001942598)
XLA Ops:
  8.7 6.6 all-to-all-start
  16.1 7.3 gather_fusion
  23.4 10.7 %convert_bitcast_fusion = bf16[16,4,128,768]{2,3,1,0:T(8,128)(2,1)} fusion(bf16[16,4,128,768]{3,2,1,0:T(8,128)(2,1)} %bitcast.32, s32[16,4,128,128]{3,2,1,0:T(8,128)} %param.10), kind=kOutput, calls=%fused_computation.5 | convolution fusion | flops 1617952768 | bytes 29360128 | tf_op jit(solution)/shard_map/ncab,ncad->ncbd/dot_general | solution.py:31
  34.1 6.7 all-to-all-start.1
  42.1 219.5 %all-to-all-done.1 = bf16[16,4,128,768]{2,3,1,0:T(8,128)(2,1)} async-done(((bf16[16,4,128,768]{2,3,1,0:T(8,128)(2,1)}), bf16[16,4,128,768]{2,3,1,0:T(8,128)(2,1)}, u32[]{:S(2)}, u32[]{:S(2)}) %all-to-all-start.1) | async-done | bytes 12582944 | tf_op jit(solution)/shard_map/all_to_all | solution.py:37
  261.7 16.7 %copy.37 = bf16[8,8,128,768]{3,1,2,0:T(8,128)(2,1)} copy(bf16[8,8,128,768]{2,3,1,0:T(8,128)(2,1)} %bitcast.19) | data formatting | bytes 25165824
  278.4 8.9 fusion.3
  288.4 234.1 %all-gather.6.cloned.1.call-done = f32[128,98304]{1,0:T(8,128)} async-done(((f32[16,98304]{1,0:T(8,128)}), f32[128,98304]{1,0:T(8,128)}) %all-gather.6.cloned.1.call-update) | async-done | bytes 50331664 | tf_op jit(solution)/shard_map/all_gather | solution.py:50
  522.4 20.2 %reduce_sum.36 = f32[16,98304]{1,0:T(8,128)} reduce(f32[8,16,98304]{2,1,0:T(8,128)} %bitcast.35, f32[]{:T(128)} %constant.7.clone.1), dimensions={0}, to_apply=%region_0.1 | reduce | flops 11010048 | bytes 56623108 | tf_op jit(solution)/shard_map/reduce_sum | solution.py:50
  542.6 5.0 reshape.69
  547.6 3.4 multiply_reduce_fusion.1
  551.0 1.2 copy-done.2
  552.6 17.4 %all-gather.4.cloned.1.call-done = bf16[2048,768]{1,0:T(8,128)(2,1)} async-done(((bf16[128,768]{1,0:T(8,128)(2,1)}), bf16[2048,768]{1,0:T(8,128)(2,1)}) %all-gather.4.cloned.1.call-update) | async-done | bytes 3145744 | tf_op jit(solution)/shard_map/all_gather | solution.py:15
  570.0 12.0 %fusion.7 = (f32[2048]{0:T(1024)S(1)}, f32[2048,2048]{0,1:T(8,128)}) fusion(bf16[2048,768]{1,0:T(8,128)(2,1)S(1)} %multiply_convert_fusion.1, bf16[2048,768]{1,0:T(8,128)(2,1)} %all-gather.4.cloned.1.call-done), kind=kOutput, calls=%fused_computation.32 | convolution fusion | flops 6446643200 | bytes 23076864 | tf_op jit(solution)/shard_map/rd,kd->rk/dot_general | solution.py:16
  582.1 8.1 fusion
  590.2 7.5 divide_convert_fusion
  597.7 7.3 convolution_convert_fusion
  605.0 7.3 gather_fusion.1
  612.3 16.6 %copy.34 = bf16[64,128,768]{1,2,0:T(8,128)(2,1)} copy(bf16[64,128,768]{2,1,0:T(8,128)(2,1)} %gather_fusion.1) | data formatting | bytes 25165824 | tf_op jit(solution)/shard_map/gather | solution.py:58
  629.0 10.6 %broadcast_select_fusion = bf16[16,4,128,768]{2,3,1,0:T(8,128)(2,1)} fusion(bf16[16,4,128,768]{2,3,1,0:T(8,128)(2,1)} %bitcast.33, pred[16,4]{1,0:T(8,128)(4,1)S(1)} %copy.33), kind=kLoop, calls=%fused_computation.6 | loop fusion | flops 6291456 | bytes 25165888 | tf_op jit(solution)/shard_map/jit(_where)/select_n | solution.py:59
  639.6 7.4 all-to-all-start.2
  647.2 1.3 constant_dynamic-slice_fusion
  648.5 1.4 copy.36
  649.9 1.8 constant_dynamic-slice_fusion.1
  651.7 215.2 %all-to-all-done.2 = bf16[16,4,128,768]{2,3,1,0:T(8,128)(2,1)} async-done(((bf16[16,4,128,768]{2,3,1,0:T(8,128)(2,1)}), bf16[16,4,128,768]{2,3,1,0:T(8,128)(2,1)}, u32[]{:S(2)}, u32[]{:S(2)}) %all-to-all-start.2) | async-done | bytes 12582944 | tf_op jit(solution)/shard_map/all_to_all | solution.py:60
  866.9 14.1 %convolution_bitcast_fusion = f32[16,4,128,768]{2,3,1,0:T(8,128)} fusion(bf16[16,4,128,768]{2,3,1,0:T(8,128)(2,1)} %all-to-all-done.2, s32[16,4,128,128]{3,2,1,0:T(8,128)} %param.10), kind=kOutput, calls=%fused_computation.7 | convolution fusion | flops 1611661312 | bytes 41943040 | tf_op jit(solution)/shard_map/ncab,ncbd->ncad/dot_general | solution.py:61
  881.0 25.1 %copy.38 = f32[8,8,128,768]{3,1,2,0:T(8,128)} copy(f32[8,8,128,768]{2,3,1,0:T(8,128)} %bitcast.30) | data formatting | bytes 50331648
  906.1 14.3 %fusion.4 = f32[16,98304]{1,0:T(8,128)} fusion(f32[64,98304]{1,0:T(8,128)} %bitcast.31, s32[64]{0:T(128)S(1)} %eq.34), kind=kOutput, calls=%fused_computation.21 | convolution fusion | flops 1207960576 | bytes 31457536 | tf_op jit(solution)/shard_map/dot_general | solution.py:65
  920.4 5.2 reshape.72
  925.6 3.4 multiply_reduce_fusion
  929.0 1.2 copy-done.3
  930.2 2.1 multiply_convert_fusion
  (38 shorter events, 5.4 us)
Async XLA Ops:
  7.2 9.0 copy-start
  8.7 25.4 %all-to-all-start = ((s32[16,1,4]{2,1,0:T(1,128)}), s32[16,1,4]{2,1,0:T(1,128)S(1)}, u32[]{:S(2)}, u32[]{:S(2)}) async-start(s32[16,1,4]{2,1,0:T(1,128)} %copy.27), calls=%async_computation | async-start | bytes 16384 | tf_op jit(solution)/shard_map/all_to_all | solution.py:38
  34.1 227.5 %all-to-all-start.1 = ((bf16[16,4,128,768]{2,3,1,0:T(8,128)(2,1)}), bf16[16,4,128,768]{2,3,1,0:T(8,128)(2,1)}, u32[]{:S(2)}, u32[]{:S(2)}) async-start(bf16[16,4,128,768]{2,3,1,0:T(8,128)(2,1)} %convert_bitcast_fusion), calls=%async_computation.1 | async-start | bytes 25165824 | tf_op jit(solution)/shard_map/all_to_all | solution.py:37
  40.8 481.7 %all-gather.6.cloned.1.call-start = ((), (), s32[]{:S(2)}) async-start(), calls=%async_computation.4 | async-start | bytes 56623104 | tf_op jit(solution)/shard_map/all_gather | solution.py:50
  287.3 282.7 %all-gather.4.cloned.1.call-start = ((), (), s32[]{:S(2)}) async-start(), calls=%async_computation.3 | async-start | bytes 3342336 | tf_op jit(solution)/shard_map/all_gather | solution.py:15
  547.6 4.6 copy-start.2
  552.6 29.5 %copy-start.5 = (bf16[2048,768]{1,0:T(8,128)(2,1)}, bf16[2048,768]{1,0:T(8,128)(2,1)S(1)}, u32[]{:S(2)}) copy-start(bf16[2048,768]{1,0:T(8,128)(2,1)S(1)} %multiply_convert_fusion.1) | copy-start | bytes 9437188
  590.2 7.5 copy-start.7
  597.7 7.3 copy-start.4
  639.6 7.4 copy-start.6
  639.6 227.3 %all-to-all-start.2 = ((bf16[16,4,128,768]{2,3,1,0:T(8,128)(2,1)}), bf16[16,4,128,768]{2,3,1,0:T(8,128)(2,1)}, u32[]{:S(2)}, u32[]{:S(2)}) async-start(bf16[16,4,128,768]{2,3,1,0:T(8,128)(2,1)} %broadcast_select_fusion), calls=%async_computation.2 | async-start | bytes 25165824 | tf_op jit(solution)/shard_map/all_to_all | solution.py:60
  920.4 11.8 %copy-start.1 = (bf16[2048,768]{1,0:T(8,128)(2,1)S(1)}, bf16[2048,768]{1,0:T(8,128)(2,1)}, u32[]{:S(2)}) copy-start(bf16[2048,768]{1,0:T(8,128)(2,1)} %param.6) | copy-start | bytes 9437188
  925.6 4.6 copy-start.3
Sparse Core Ops, SparseCore 0:
  287.4 234.9 all-gather.5
  524.6 45.3 all-gather.3
